TPU v7x, 32 devices: a whole 2x2x4 slice. The times are simulated.
32 devices in a mesh: batch: 2 (over y), row: 4 (over x, core), col: 4 (over z).
Axes of the slice: x: 2, y: 2, z: 4, core: 2. Of those that a mesh axis runs over, the one named last changes fastest.
Arguments:
- patches: bfloat16 [2, 4096, 1280], P('batch', 'col', 'row'), may hold values from -6 to 6
- qkv_weight: bfloat16 [1280, 3, 1280], P('row', None, 'col'), may hold values from -0.15625 to 0.15625
- qv_bias: float32 [2, 1280], P(None, 'col'), may hold values from -0.6 to 0.6
- proj_weight: bfloat16 [1280, 1280], P('col', 'row'), may hold values from -2.5 to 2.5
- proj_bias: float32 [1280], P('row'), may hold values from -1.2 to 1.2
- norm1_gain: float32 [1280], P('row'), may hold values from 0.5 to 1.5
- norm1_shift: float32 [1280], P('row'), may hold values from -1.2 to 1.2
- norm2_gain: float32 [1280], P('row'), may hold values from 0.5 to 1.5
- norm2_shift: float32 [1280], P('row'), may hold values from -1.2 to 1.2
- fc1_weight: bfloat16 [1280, 5120], P('row', 'col'), may hold values from -0.15625 to 0.15625
- fc1_bias: float32 [5120], P('col'), may hold values from -1.2 to 1.2
- fc2_weight: bfloat16 [5120, 1280], P('col', 'row'), may hold values from -0.078125 to 0.078125
- fc2_bias: float32 [1280], P('row'), may hold values from -1.2 to 1.2
- height_table: bfloat16 [127, 80], replicated, may hold values from -0.625 to 0.625
- width_table: bfloat16 [127, 80], replicated, may hold values from -0.625 to 0.625
- out_grad: bfloat16 [2, 4096, 1280], P('batch', 'col', 'row'), may hold values from -6 to 6
Outputs:
- block_out: bfloat16 [2, 4096, 1280], P('batch', 'col', 'row')
- patches_grad: float32 [2, 4096, 1280], P('batch', 'col', 'row')
- qkv_weight_grad: float32 [1280, 3, 1280], P('row', None, 'col')
- qv_bias_grad: float32 [2, 1280], P(None, 'col')
- proj_weight_grad: float32 [1280, 1280], P('col', 'row')
- proj_bias_grad: float32 [1280], P('row')
- norm1_gain_grad: float32 [1280], P('row')
- norm1_shift_grad: float32 [1280], P('row')
- norm2_gain_grad: float32 [1280], P('row')
- norm2_shift_grad: float32 [1280], P('row')
- fc1_weight_grad: float32 [1280, 5120], P('row', 'col')
- fc1_bias_grad: float32 [5120], P('col')
- fc2_weight_grad: float32 [5120, 1280], P('col', 'row')
- fc2_bias_grad: float32 [1280], P('row')
- height_table_grad: float32 [127, 80], replicated
- width_table_grad: float32 [127, 80], replicated
All inputs are finite; a program needn't handle non-finite values.
Results may differ from a plain program's by a relative error of at most 0.012.
Values may be sent and summed in bfloat16 or wider, within the bound.
A program may use at most 256 MiB of HBM per device.

v0:
```python
from functools import partial
import jax
import jax.numpy as jnp
from jax import lax
from jax.sharding import PartitionSpec as P

D = 1280
HEAD_DIM = 80
GRID = 64
EPSILON = 1e-06
HIGHEST = lax.Precision.HIGHEST


def feature_sums(first, second):
    return lax.psum((first, second), "row")


def rows_over_col(values):
    return lax.all_gather(values, "col", axis=0, tiled=True)


def rows_over_row(values):
    return lax.all_gather(values, "row", axis=0, tiled=True)


def sum_over_row(values):
    return lax.psum_scatter(values, "row", scatter_dimension=0, tiled=True)


def sum_over_col(values):
    return lax.psum_scatter(values, "col", scatter_dimension=0, tiled=True)


def gather_key_value(key_local, value_local):
    couple = jnp.stack([key_local, value_local], 1).astype(jnp.bfloat16)
    couple_full = lax.all_gather(couple, "row", axis=0, tiled=True)
    return (couple_full[:, 0], couple_full[:, 1])


def normalize(values, norm_gain, norm_shift, model_width):
    first, second = feature_sums(jnp.sum(values, -1), jnp.sum(values * values, -1))
    center = first / model_width
    inv_scale = lax.rsqrt(second / model_width - center * center + EPSILON)
    scaled = (values - center[:, None]) * inv_scale[:, None]
    return (scaled, inv_scale, (scaled * norm_gain + norm_shift).astype(jnp.bfloat16))


def normalize_back(grad_in, scaled, inv_scale, norm_gain, model_width):
    scaled_grad = grad_in * norm_gain
    first, second = feature_sums(jnp.sum(scaled_grad, -1), jnp.sum(scaled_grad * scaled, -1))
    return inv_scale[:, None] * (
        scaled_grad - first[:, None] / model_width - scaled * (second[:, None] / model_width)
    )


def select_table(row_count, col_count, offset, grid_side):
    shape = (row_count, col_count, 2 * grid_side - 1)
    first = lax.broadcasted_iota(jnp.int32, shape, 0) + offset
    second = lax.broadcasted_iota(jnp.int32, shape, 1)
    third = lax.broadcasted_iota(jnp.int32, shape, 2)
    return (first - second + grid_side - 1 == third).astype(jnp.bfloat16)


def head_scores(query_one, key_one, row_select, col_select, score_scale, grid_side):
    query_lines = query_one.shape[0] // grid_side
    query_grid = query_one.reshape(query_lines, grid_side, query_one.shape[1])
    rel_rows = jnp.einsum(
        "hwc,hkc->hwk", query_grid, row_select, preferred_element_type=jnp.float32
    )
    rel_cols = jnp.einsum(
        "hwc,wkc->hwk", query_grid, col_select, preferred_element_type=jnp.float32
    )
    position = (rel_rows[:, :, :, None] + rel_cols[:, :, None, :]).reshape(
        query_one.shape[0], grid_side * grid_side
    )
    raw = jnp.einsum("qc,kc->qk", query_one, key_one, preferred_element_type=jnp.float32)
    return raw * score_scale + position


def shards(
    patches,
    qkv_weight,
    qv_bias,
    proj_weight,
    proj_bias,
    norm1_gain,
    norm1_shift,
    norm2_gain,
    norm2_shift,
    fc1_weight,
    fc1_bias,
    fc2_weight,
    fc2_bias,
    height_table,
    width_table,
    out_grad,
):
    grid_side = GRID
    model_width = D
    head_size = HEAD_DIM
    score_scale = head_size ** (-0.5)
    local_cols = qkv_weight.shape[2]
    head_count = local_cols // head_size
    image_tokens = grid_side * grid_side
    query_rows = image_tokens // lax.axis_size("row")
    query_lines = query_rows // grid_side
    residual = patches[0].astype(jnp.float32)
    scaled1, inv_scale1, normed1 = normalize(residual, norm1_gain, norm1_shift, model_width)
    gathered1 = rows_over_col(normed1)
    partial_qkv = jnp.einsum(
        "lf,fkh->lkh", gathered1, qkv_weight, preferred_element_type=jnp.float32
    )
    local_qkv = sum_over_row(partial_qkv)
    queries = local_qkv[:, 0] + qv_bias[0]
    key_full, value_full = gather_key_value(local_qkv[:, 1], local_qkv[:, 2] + qv_bias[1])
    queries = queries.astype(jnp.bfloat16)
    row_onehot = select_table(
        query_lines, grid_side, lax.axis_index("row") * query_lines, grid_side
    )
    col_onehot = select_table(grid_side, grid_side, 0, grid_side)
    row_select = jnp.einsum(
        "ijd,dc->ijc", row_onehot, height_table, preferred_element_type=jnp.float32
    ).astype(jnp.bfloat16)
    col_select = jnp.einsum(
        "ijd,dc->ijc", col_onehot, width_table, preferred_element_type=jnp.float32
    ).astype(jnp.bfloat16)

    def split_heads(values):
        return values.reshape(values.shape[0], head_count, head_size).transpose(1, 0, 2)

    def join_heads(values):
        return values.transpose(1, 0, 2).reshape(values.shape[1], head_count * head_size)

    query_heads = split_heads(queries)
    key_heads = split_heads(key_full)
    value_heads = split_heads(value_full)

    def attend(operands):
        query_one, key_one, value_one = operands
        scores = head_scores(query_one, key_one, row_select, col_select, score_scale, grid_side)
        row_max = jnp.max(scores, -1, keepdims=True)
        raw_weights = jnp.exp(scores - row_max)
        row_total = jnp.sum(raw_weights, -1, keepdims=True)
        weights = (raw_weights / row_total).astype(jnp.bfloat16)
        result = jnp.dot(weights, value_one, preferred_element_type=jnp.float32).astype(
            jnp.bfloat16
        )
        return (result, (row_max + jnp.log(row_total))[:, 0])

    attended, log_total = lax.map(attend, (query_heads, key_heads, value_heads))
    merged = join_heads(attended)
    gathered_attn = rows_over_row(merged)
    projected = sum_over_col(
        jnp.dot(gathered_attn, proj_weight, preferred_element_type=jnp.float32)
    )
    middle = residual + (projected + proj_bias)
    scaled2, inv_scale2, normed2 = normalize(middle, norm2_gain, norm2_shift, model_width)
    gathered2 = rows_over_col(normed2)
    preact = (
        sum_over_row(jnp.dot(gathered2, fc1_weight, preferred_element_type=jnp.float32)) + fc1_bias
    )
    activated = jax.nn.gelu(preact, approximate=False).astype(jnp.bfloat16)
    gathered_act = rows_over_row(activated)
    lowered = sum_over_col(jnp.dot(gathered_act, fc2_weight, preferred_element_type=jnp.float32))
    final = middle + (lowered + fc2_bias)
    cotangent = out_grad[0]
    cot_all = rows_over_col(cotangent)
    fc2_grad, fc2_bias_grad = (
        jnp.einsum("lh,lf->hf", gathered_act, cot_all, preferred_element_type=jnp.float32),
        jnp.sum(cot_all, 0, dtype=jnp.float32),
    )
    act_grad = sum_over_row(
        jnp.einsum("lf,hf->lh", cot_all, fc2_weight, preferred_element_type=jnp.float32)
    )
    gelu_fn = partial(jax.nn.gelu, approximate=False)
    unused, gelu_back = jax.vjp(gelu_fn, preact)
    preact_grad = gelu_back(act_grad)[0].astype(jnp.bfloat16)
    preact_all = rows_over_row(preact_grad)
    fc1_grad, fc1_bias_grad = (
        jnp.einsum("lf,lh->fh", gathered2, preact_all, preferred_element_type=jnp.float32),
        jnp.sum(preact_all, 0, dtype=jnp.float32),
    )
    normed2_grad = sum_over_col(
        jnp.einsum("lh,fh->lf", preact_all, fc1_weight, preferred_element_type=jnp.float32)
    )
    gain2_part = jnp.sum(normed2_grad * scaled2, 0)
    shift2_part = jnp.sum(normed2_grad, 0)
    middle_grad = cotangent.astype(jnp.float32) + normalize_back(
        normed2_grad, scaled2, inv_scale2, norm2_gain, model_width
    )
    branch_grad = middle_grad.astype(jnp.bfloat16)
    branch_all = rows_over_col(branch_grad)
    proj_grad, proj_bias_grad = (
        jnp.einsum("lh,lf->hf", gathered_attn, branch_all, preferred_element_type=jnp.float32),
        jnp.sum(branch_all, 0, dtype=jnp.float32),
    )
    merged_grad = sum_over_row(
        jnp.einsum("lf,hf->lh", branch_all, proj_weight, preferred_element_type=jnp.float32)
    ).astype(jnp.bfloat16)
    merged_grad_heads = split_heads(merged_grad)

    def attend_back(operands):
        query_one, key_one, value_one, grad_one, total_one = operands
        scores = head_scores(query_one, key_one, row_select, col_select, score_scale, grid_side)
        weights = jnp.exp(scores - total_one[:, None])
        weight_grad = jnp.einsum(
            "qc,kc->qk", grad_one, value_one, preferred_element_type=jnp.float32
        )
        row_inner = jnp.sum(weights * weight_grad, -1, keepdims=True)
        score_grad = (weights * (weight_grad - row_inner)).astype(jnp.bfloat16)
        value_part = jnp.einsum(
            "qk,qc->kc", weights.astype(jnp.bfloat16), grad_one, preferred_element_type=jnp.float32
        )
        key_part = (
            jnp.einsum("qk,qc->kc", score_grad, query_one, preferred_element_type=jnp.float32)
            * score_scale
        )
        query_part = jnp.dot(score_grad, key_one, preferred_element_type=jnp.float32) * score_scale
        grid_form = score_grad.astype(jnp.float32).reshape(
            query_lines, grid_side, grid_side, grid_side
        )
        row_grad = jnp.sum(grid_form, 3)
        col_grad = jnp.sum(grid_form, 2)
        query_grid = query_one.astype(jnp.float32).reshape(query_lines, grid_side, head_size)
        from_rows = jnp.einsum(
            "hwk,hkc->hwc", row_grad, row_select.astype(jnp.float32), precision=HIGHEST
        )
        from_cols = jnp.einsum(
            "hwk,wkc->hwc", col_grad, col_select.astype(jnp.float32), precision=HIGHEST
        )
        query_part = query_part + (from_rows + from_cols).reshape(query_rows, head_size)
        row_select_grad = jnp.einsum("hwk,hwc->hkc", row_grad, query_grid, precision=HIGHEST)
        col_select_grad = jnp.einsum("hwk,hwc->wkc", col_grad, query_grid, precision=HIGHEST)
        return (query_part, key_part, value_part, row_select_grad, col_select_grad)

    query_parts, key_parts, value_parts, row_sel_grads, col_sel_grads = lax.map(
        attend_back, (query_heads, key_heads, value_heads, merged_grad_heads, log_total)
    )
    kv_grad = sum_over_row(jnp.stack([join_heads(key_parts), join_heads(value_parts)], 1)).astype(
        jnp.bfloat16
    )
    query_grad = join_heads(query_parts).astype(jnp.bfloat16)
    qkv_grad_local = jnp.concatenate([query_grad[:, None], kv_grad], 1)
    qkv_all = rows_over_row(qkv_grad_local)
    qkv_grad, qv_bias_grad = (
        jnp.einsum("lf,lkh->fkh", gathered1, qkv_all, preferred_element_type=jnp.float32),
        jnp.stack(
            [
                jnp.sum(qkv_all[:, 0], 0, dtype=jnp.float32),
                jnp.sum(qkv_all[:, 2], 0, dtype=jnp.float32),
            ],
            0,
        ),
    )
    normed1_grad = sum_over_col(
        jnp.einsum("lkh,fkh->lf", qkv_all, qkv_weight, preferred_element_type=jnp.float32)
    )
    gain1_part = jnp.sum(normed1_grad * scaled1, 0)
    shift1_part = jnp.sum(normed1_grad, 0)
    input_grad = middle_grad + normalize_back(
        normed1_grad, scaled1, inv_scale1, norm1_gain, model_width
    )
    height_part = jnp.einsum(
        "ijd,ijc->dc", row_onehot.astype(jnp.float32), jnp.sum(row_sel_grads, 0), precision=HIGHEST
    )
    width_part = jnp.einsum(
        "ijd,ijc->dc", col_onehot.astype(jnp.float32), jnp.sum(col_sel_grads, 0), precision=HIGHEST
    )
    gain1_grad, shift1_grad, gain2_grad, shift2_grad = lax.psum(
        (gain1_part, shift1_part, gain2_part, shift2_part), ("batch", "col")
    )
    height_grad, width_grad = lax.psum((height_part, width_part), ("batch", "row", "col"))
    (
        qkv_grad,
        qv_bias_grad,
        proj_grad,
        proj_bias_grad,
        fc1_grad,
        fc1_bias_grad,
        fc2_grad,
        fc2_bias_grad,
    ) = (
        lax.psum(qkv_grad.astype(jnp.bfloat16), "batch").astype(jnp.float32),
        lax.psum(qv_bias_grad.astype(jnp.bfloat16), "batch").astype(jnp.float32),
        lax.psum(proj_grad.astype(jnp.bfloat16), "batch").astype(jnp.float32),
        lax.psum(proj_bias_grad.astype(jnp.bfloat16), "batch").astype(jnp.float32),
        lax.psum(fc1_grad.astype(jnp.bfloat16), "batch").astype(jnp.float32),
        lax.psum(fc1_bias_grad.astype(jnp.bfloat16), "batch").astype(jnp.float32),
        lax.psum(fc2_grad.astype(jnp.bfloat16), "batch").astype(jnp.float32),
        lax.psum(fc2_bias_grad.astype(jnp.bfloat16), "batch").astype(jnp.float32),
    )
    return (
        final[None].astype(jnp.bfloat16),
        input_grad[None],
        qkv_grad,
        qv_bias_grad,
        proj_grad,
        proj_bias_grad,
        gain1_grad,
        shift1_grad,
        gain2_grad,
        shift2_grad,
        fc1_grad,
        fc1_bias_grad,
        fc2_grad,
        fc2_bias_grad,
        height_grad,
        width_grad,
    )


def solution(mesh):
    in_specs = (
        P("batch", "col", "row"),
        P("row", None, "col"),
        P(None, "col"),
        P("col", "row"),
        P("row"),
        P("row"),
        P("row"),
        P("row"),
        P("row"),
        P("row", "col"),
        P("col"),
        P("col", "row"),
        P("row"),
        P(),
        P(),
        P("batch", "col", "row"),
    )
    out_specs = (
        P("batch", "col", "row"),
        P("batch", "col", "row"),
        P("row", None, "col"),
        P(None, "col"),
        P("col", "row"),
        P("row"),
        P("row"),
        P("row"),
        P("row"),
        P("row"),
        P("row", "col"),
        P("col"),
        P("col", "row"),
        P("row"),
        P(),
        P(),
    )
    return jax.shard_map(shards, mesh=mesh, in_specs=in_specs, out_specs=out_specs, check_vma=False)
```

profile of v0, /device:TPU:8, one launch (start us, length us, event | category | flops | bytes accessed | tf_op | source)
XLA Modules:
  0.0 2642.6 jit_solution(13296211281150519857)
XLA Ops:
  19.7 53.3 %all-gather.11.cloned.1.call-done = bf16[4096,320]{0,1:T(8,128)(2,1)} async-done(((bf16[1024,320]{0,1:T(8,128)(2,1)}), bf16[4096,320]{0,1:T(8,128)(2,1)}) %all-gather.11.cloned.1.call-update) | async-done | bytes 2621456 | tf_op jit(solution)/shard_map/all_gather | solution.py:19
  85.4 119.9 %reduce-scatter.10.cloned.1.call-done = f32[1024,3,320]{0,2,1:T(8,128)} async-done(((f32[4096,3,320]{0,2,1:T(8,128)}), f32[1024,3,320]{0,2,1:T(8,128)}) %reduce-scatter.10.cloned.1.call-update) | async-done | bytes 3932176 | tf_op jit(solution)/shard_map/reduce_scatter | solution.py:27
  218.2 33.4 %all-gather.13.cloned.1.call-done = bf16[4096,2,320]{0,2,1:T(8,128)(2,1)} async-done(((bf16[1024,2,320]{0,2,1:T(8,128)(2,1)}), bf16[4096,2,320]{0,2,1:T(8,128)(2,1)}) %all-gather.13.cloned.1.call-update) | async-done | bytes 5242896 | tf_op jit(solution)/shard_map/all_gather | solution.py:36
  268.2 293.5 %while.30 = (s32[]{:T(128)}, bf16[4,1024,80]{1,2,0:T(8,128)(2,1)S(1)}, f32[4,1024]{1,0:T(4,128)}, bf16[4,1024,80]{2,1,0:T(8,128)(2,1)}, bf16[4,4096,80]{2,1,0:T(...) while((s32[]{:T(128)}, ...), condition=%wide.region_8.9_spmd, body=%wide.region_5.8_spmd.sunk | while | flops 1400978432 | bytes 123054200 | solution.py:150
  281.7 27.9 %add.329 = f32[1024,4096]{1,0:T(8,128)} reshape(f32[16,64,64,64]{3,2,1,0:T(8,128)} %broadcast_add_fusion.4) | data formatting | bytes 33554432 | tf_op jit(solution)/shard_map/while/body/eval_jaxpr/add | solution.py:73
  309.6 14.6 fusion.193
  355.1 27.9 %add.329 = f32[1024,4096]{1,0:T(8,128)} reshape(f32[16,64,64,64]{3,2,1,0:T(8,128)} %broadcast_add_fusion.4) | data formatting | bytes 33554432 | tf_op jit(solution)/shard_map/while/body/eval_jaxpr/add | solution.py:73
  383.0 14.6 fusion.193
  428.4 27.9 %add.329 = f32[1024,4096]{1,0:T(8,128)} reshape(f32[16,64,64,64]{3,2,1,0:T(8,128)} %broadcast_add_fusion.4) | data formatting | bytes 33554432 | tf_op jit(solution)/shard_map/while/body/eval_jaxpr/add | solution.py:73
  456.3 14.6 fusion.193
  501.8 27.9 %add.329 = f32[1024,4096]{1,0:T(8,128)} reshape(f32[16,64,64,64]{3,2,1,0:T(8,128)} %broadcast_add_fusion.4) | data formatting | bytes 33554432 | tf_op jit(solution)/shard_map/while/body/eval_jaxpr/add | solution.py:73
  529.7 14.6 fusion.193
  562.8 25.5 all-gather.15.cloned.1.call-done
  594.5 93.3 %reduce-scatter.12.cloned.1.call-done = f32[1024,320]{0,1:T(8,128)} async-done(((f32[4096,320]{0,1:T(8,128)}), f32[1024,320]{0,1:T(8,128)}) %reduce-scatter.12.cloned.1.call-update) | async-done | bytes 1310736 | tf_op jit(solution)/shard_map/reduce_scatter | solution.py:31
  700.1 42.7 %all-gather.27.cloned.1.call-done = bf16[1,4096,320]{1,2,0:T(8,128)(2,1)} async-done(((bf16[1,1024,320]{1,2,0:T(8,128)(2,1)}), bf16[1,4096,320]{1,2,0:T(8,128)(2,1)}) %all-gather.27.cloned.1.call-update) | async-done | bytes 2621456 | tf_op jit(solution)/shard_map/all_gather | solution.py:19
  754.6 43.9 %all-gather.17.cloned.1.call-done = bf16[4096,320]{0,1:T(8,128)(2,1)} async-done(((bf16[1024,320]{0,1:T(8,128)(2,1)}), bf16[4096,320]{0,1:T(8,128)(2,1)}) %all-gather.17.cloned.1.call-update) | async-done | bytes 2621456 | tf_op jit(solution)/shard_map/all_gather | solution.py:19
  812.8 142.1 %reduce-scatter.18.cloned.1.call-done = f32[1024,1280]{1,0:T(8,128)} async-done(((f32[4096,1280]{1,0:T(8,128)}), f32[1024,1280]{1,0:T(8,128)}) %reduce-scatter.18.cloned.1.call-update) | async-done | bytes 5242896 | tf_op jit(solution)/shard_map/reduce_scatter | solution.py:27
  954.9 155.9 %reduce-scatter.14.cloned.1.call-done = f32[1024,1280]{1,0:T(8,128)} async-done(((f32[4096,1280]{1,0:T(8,128)}), f32[1024,1280]{1,0:T(8,128)}) %reduce-scatter.14.cloned.1.call-update) | async-done | bytes 5242896 | tf_op jit(solution)/shard_map/reduce_scatter | solution.py:27
  1110.8 15.3 add_convert_fusion
  1126.2 70.3 %all-gather.21.cloned.1.call-done = bf16[4096,1280]{1,0:T(8,128)(2,1)} async-done(((bf16[1024,1280]{1,0:T(8,128)(2,1)}), bf16[4096,1280]{1,0:T(8,128)(2,1)}) %all-gather.21.cloned.1.call-update) | async-done | bytes 10485776 | tf_op jit(solution)/shard_map/all_gather | solution.py:23
  1209.2 93.9 %reduce-scatter.20.cloned.1.call-done = f32[1024,320]{0,1:T(8,128)} async-done(((f32[4096,320]{0,1:T(8,128)}), f32[1024,320]{0,1:T(8,128)}) %reduce-scatter.20.cloned.1.call-update) | async-done | bytes 1310736 | tf_op jit(solution)/shard_map/reduce_scatter | solution.py:31
  1316.0 52.7 %all-gather.23.cloned.1.call-done = bf16[4096,320]{0,1:T(8,128)(2,1)} async-done(((bf16[1024,320]{0,1:T(8,128)(2,1)}), bf16[4096,320]{0,1:T(8,128)(2,1)}) %all-gather.23.cloned.1.call-update) | async-done | bytes 2621456 | tf_op jit(solution)/shard_map/all_gather | solution.py:19
  1374.4 52.1 %reduce-scatter.22.cloned.1.call-done = f32[1024,320]{0,1:T(8,128)} async-done(((f32[4096,320]{0,1:T(8,128)}), f32[1024,320]{0,1:T(8,128)}) %reduce-scatter.22.cloned.1.call-update) | async-done | bytes 1310736 | tf_op jit(solution)/shard_map/reduce_scatter | solution.py:27
  1429.1 574.5 %while.31 = (s32[]{:T(128)}, bf16[4,1024,80]{1,2,0:T(8,128)(2,1)}, f32[4,4096,80]{1,2,0:T(8,128)}, f32[4,4096,80]{1,2,0:T(8,128)}, f32[4,16,64,80]{3,2,1,0:T(8,1...) while((s32[]{:T(128)}, bf16[4,1024,80]{1,2,0:T(8,128)(2,1)}, ...), condition=%wide.region_27.28_spmd, body=%wide.region_23.27_spmd.sunk | while | flops 3678845952 | bytes 353068224 | solution.py:236
  1453.0 27.9 %add.336 = f32[1024,4096]{1,0:T(8,128)} reshape(f32[16,64,64,64]{3,2,1,0:T(8,128)} %broadcast_add_fusion.5) | data formatting | bytes 33554432 | tf_op jit(solution)/shard_map/while/body/eval_jaxpr/add | solution.py:73
  1480.9 16.5 multiply_reduce_fusion.7
  1520.3 24.0 reshape.157
  1544.3 15.4 fusion.218
  1596.6 27.9 %add.336 = f32[1024,4096]{1,0:T(8,128)} reshape(f32[16,64,64,64]{3,2,1,0:T(8,128)} %broadcast_add_fusion.5) | data formatting | bytes 33554432 | tf_op jit(solution)/shard_map/while/body/eval_jaxpr/add | solution.py:73
  1624.5 16.5 multiply_reduce_fusion.7
  1663.8 24.0 reshape.157
  1687.8 15.4 fusion.218
  1740.1 27.9 %add.336 = f32[1024,4096]{1,0:T(8,128)} reshape(f32[16,64,64,64]{3,2,1,0:T(8,128)} %broadcast_add_fusion.5) | data formatting | bytes 33554432 | tf_op jit(solution)/shard_map/while/body/eval_jaxpr/add | solution.py:73
  1768.0 16.5 multiply_reduce_fusion.7
  1807.3 24.0 reshape.157
  1831.3 15.4 fusion.218
  1883.5 27.9 %add.336 = f32[1024,4096]{1,0:T(8,128)} reshape(f32[16,64,64,64]{3,2,1,0:T(8,128)} %broadcast_add_fusion.5) | data formatting | bytes 33554432 | tf_op jit(solution)/shard_map/while/body/eval_jaxpr/add | solution.py:73
  1911.4 16.5 multiply_reduce_fusion.7
  1950.7 24.0 reshape.157
  1974.7 15.4 fusion.218
  2019.9 78.4 %reduce-scatter.24.cloned.1.call-done = f32[1024,2,320]{0,2,1:T(8,128)} async-done(((f32[4096,2,320]{0,2,1:T(8,128)}), f32[1024,2,320]{0,2,1:T(8,128)}) %reduce-scatter.24.cloned.1.call-update) | async-done | bytes 2621456 | tf_op jit(solution)/shard_map/reduce_scatter | solution.py:27
  2111.5 58.5 %all-gather.19.cloned.1.call-done = bf16[4096,1280]{1,0:T(8,128)(2,1)} async-done(((bf16[1024,1280]{1,0:T(8,128)(2,1)}), bf16[4096,1280]{1,0:T(8,128)(2,1)}) %all-gather.19.cloned.1.call-update) | async-done | bytes 10485776 | tf_op jit(solution)/shard_map/all_gather | solution.py:23
  2179.6 47.3 %all-gather.25.cloned.1.call-done = bf16[4096,3,320]{0,2,1:T(8,128)(2,1)} async-done(((bf16[1024,3,320]{0,2,1:T(8,128)(2,1)}), bf16[4096,3,320]{0,2,1:T(8,128)(2,1)}) %all-gather.25.cloned.1.call-update) | async-done | bytes 7864336 | tf_op jit(solution)/shard_map/all_gather | solution.py:23
  2285.6 25.0 all-reduce.13.cloned.1.call-done
  2318.5 88.2 %reduce-scatter.26.cloned.1.call-done = f32[1024,320]{0,1:T(8,128)} async-done(((f32[4096,320]{0,1:T(8,128)}), f32[1024,320]{0,1:T(8,128)}) %reduce-scatter.26.cloned.1.call-update) | async-done | bytes 1310736 | tf_op jit(solution)/shard_map/reduce_scatter | solution.py:31
  2415.5 87.7 %reduce-scatter.16.cloned.1.call-done = f32[1024,320]{0,1:T(8,128)} async-done(((f32[4096,320]{0,1:T(8,128)}), f32[1024,320]{0,1:T(8,128)}) %reduce-scatter.16.cloned.1.call-update) | async-done | bytes 1310736 | tf_op jit(solution)/shard_map/reduce_scatter | solution.py:31
  2507.6 19.1 all-reduce.1
  2526.7 106.0 %all-reduce.11.cloned.1.call-done = (f32[127,80]{0,1:T(8,128)}, f32[127,80]{0,1:T(8,128)}) async-done(((f32[127,80]{0,1:T(8,128)}, f32[127,80]{0,1:T(8,128)}), (f32[127,80]{0,1:T(8,128)}, f32[127,80]{0,1:T(8,128)})) %all-reduce.11.cloned.1.call-update) | async-done | bytes 81296 | tf_op jit(solution)/shard_map/psum | solution.py:272
  (322 shorter events, 617.2 us)
Async XLA Ops:
  7.2 791.3 %copy-start = (bf16[320,1280]{1,0:T(8,128)(2,1)S(1)}, bf16[320,1280]{1,0:T(8,128)(2,1)}, u32[]{:S(2)}) copy-start(bf16[320,1280]{1,0:T(8,128)(2,1)} %param.29) | copy-start | bytes 2457604
  7.2 65.8 %all-gather.11.cloned.1.call-start = ((), (), s32[]{:S(2)}) async-start(), calls=%async_computation.9 | async-start | bytes 3276800 | tf_op jit(solution)/shard_map/all_gather | solution.py:19
  19.7 185.7 %reduce-scatter.10.cloned.1.call-start = ((), (), s32[]{:S(2)}) async-start(), calls=%async_computation.10 | async-start | bytes 19660800 | tf_op jit(solution)/shard_map/reduce_scatter | solution.py:27
  84.7 126.9 %copy-start.44 = (bf16[127,80]{0,1:T(8,128)(2,1)S(1)}, bf16[127,80]{0,1:T(8,128)(2,1)}, u32[]{:S(2)}) copy-start(bf16[127,80]{0,1:T(8,128)(2,1)} %param.33) | copy-start | bytes 60964
  84.7 127.2 %copy-start.45 = (bf16[127,80]{0,1:T(8,128)(2,1)S(1)}, bf16[127,80]{0,1:T(8,128)(2,1)}, u32[]{:S(2)}) copy-start(bf16[127,80]{0,1:T(8,128)(2,1)} %param.34) | copy-start | bytes 60964
  84.7 166.8 %all-gather.13.cloned.1.call-start = ((), (), s32[]{:S(2)}) async-start(), calls=%async_computation.11 | async-start | bytes 6553600 | tf_op jit(solution)/shard_map/all_gather | solution.py:36
  211.0 377.3 %all-gather.15.cloned.1.call-start = ((), (), s32[]{:S(2)}) async-start(), calls=%async_computation.12 | async-start | bytes 3276800 | tf_op jit(solution)/shard_map/all_gather | solution.py:23
  268.2 320.1 %copy-start.13 = (bf16[320,320]{1,0:T(8,128)(2,1)S(1)}, bf16[320,320]{1,0:T(8,128)(2,1)}, u32[]{:S(2)}) copy-start(bf16[320,320]{1,0:T(8,128)(2,1)} %param.23) | copy-start | bytes 614404
  562.6 125.3 %reduce-scatter.12.cloned.1.call-start = ((), (), s32[]{:S(2)}) async-start(), calls=%async_computation.13 | async-start | bytes 6553600 | tf_op jit(solution)/shard_map/reduce_scatter | solution.py:31
  593.9 93.9 %copy-start.5 = (bf16[1,1024,320]{1,2,0:T(8,128)(2,1)S(1)}, bf16[1,1024,320]{1,2,0:T(8,128)(2,1)}, u32[]{:S(2)}) copy-start(bf16[1,1024,320]{1,2,0:T(8,128)(2,1)} %param.20) | copy-start | bytes 1966084
  593.9 94.0 %copy-start.40 = (f32[320]{0:T(512)S(1)}, f32[320]{0:T(512)}, u32[]{:S(2)}) copy-start(f32[320]{0:T(512)} %param.24) | copy-start | bytes 3844
  593.9 103.7 %copy-start.31 = (f32[320]{0:T(512)S(1)}, f32[320]{0:T(512)}, u32[]{:S(2)}) copy-start(f32[320]{0:T(512)} %param.27) | copy-start | bytes 3844
  593.9 103.7 %copy-start.41 = (f32[320]{0:T(512)S(1)}, f32[320]{0:T(512)}, u32[]{:S(2)}) copy-start(f32[320]{0:T(512)} %param.28) | copy-start | bytes 3844
  593.9 148.9 %all-gather.27.cloned.1.call-start = ((), (), s32[]{:S(2)}) async-start(), calls=%async_computation.26 | async-start | bytes 3276800 | tf_op jit(solution)/shard_map/all_gather | solution.py:19
  594.5 204.0 %all-gather.17.cloned.1.call-start = ((), (), s32[]{:S(2)}) async-start(), calls=%async_computation.14 | async-start | bytes 3276800 | tf_op jit(solution)/shard_map/all_gather | solution.py:19
  697.5 615.4 %copy-start.19 = (f32[1024]{0:T(1024)}, f32[1024]{0:T(1024)S(1)}, u32[]{:S(2)}) copy-start(f32[1024]{0:T(1024)S(1)} %get-tuple-element.230) | copy-start | bytes 12292
  697.5 615.4 %copy-start.21 = (f32[1024]{0:T(1024)}, f32[1024]{0:T(1024)S(1)}, u32[]{:S(2)}) copy-start(f32[1024]{0:T(1024)S(1)} %get-tuple-element.231) | copy-start | bytes 12292
  700.0 254.9 %reduce-scatter.18.cloned.1.call-start = ((), (), s32[]{:S(2)}) async-start(), calls=%async_computation.18 | async-start | bytes 26214400 | tf_op jit(solution)/shard_map/reduce_scatter | solution.py:27
  754.5 356.3 %reduce-scatter.14.cloned.1.call-start = ((), (), s32[]{:S(2)}) async-start(), calls=%async_computation.15 | async-start | bytes 26214400 | tf_op jit(solution)/shard_map/reduce_scatter | solution.py:27
  812.7 298.1 %copy-start.33 = (f32[1280]{0:T(1024)S(1)}, f32[1280]{0:T(1024)}, u32[]{:S(2)}) copy-start(f32[1280]{0:T(1024)} %param.30) | copy-start | bytes 15364
  812.7 383.8 %all-gather.21.cloned.1.call-start = ((), (), s32[]{:S(2)}) async-start(), calls=%async_computation.19 | async-start | bytes 13107200 | tf_op jit(solution)/shard_map/all_gather | solution.py:23
  1126.1 176.9 %reduce-scatter.20.cloned.1.call-start = ((), (), s32[]{:S(2)}) async-start(), calls=%async_computation.20 | async-start | bytes 6553600 | tf_op jit(solution)/shard_map/reduce_scatter | solution.py:31
  1209.1 103.8 %copy-start.10 = (bf16[1,1024,320]{1,2,0:T(8,128)(2,1)S(1)}, bf16[1,1024,320]{1,2,0:T(8,128)(2,1)}, u32[]{:S(2)}) copy-start(bf16[1,1024,320]{1,2,0:T(8,128)(2,1)} %param.35) | copy-start | bytes 1966084
  1209.1 159.5 %all-gather.23.cloned.1.call-start = ((), (), s32[]{:S(2)}) async-start(), calls=%async_computation.21 | async-start | bytes 3276800 | tf_op jit(solution)/shard_map/all_gather | solution.py:19
  1315.9 110.5 %reduce-scatter.22.cloned.1.call-start = ((), (), s32[]{:S(2)}) async-start(), calls=%async_computation.22 | async-start | bytes 6553600 | tf_op jit(solution)/shard_map/reduce_scatter | solution.py:27
  1374.3 724.1 %reduce-scatter.24.cloned.1.call-start = ((), (), s32[]{:S(2)}) async-start(), calls=%async_computation.23 | async-start | bytes 13107200 | tf_op jit(solution)/shard_map/reduce_scatter | solution.py:27
  2012.9 157.2 %all-gather.19.cloned.1.call-start = ((), (), s32[]{:S(2)}) async-start(), calls=%async_computation.16 | async-start | bytes 13107200 | tf_op jit(solution)/shard_map/all_gather | solution.py:23
  2019.9 80.4 %copy-start.18 = (bf16[4,1024,80]{1,2,0:T(8,128)(2,1)S(1)}, bf16[4,1024,80]{1,2,0:T(8,128)(2,1)}, u32[]{:S(2)}) copy-start(bf16[4,1024,80]{1,2,0:T(8,128)(2,1)} %get-tuple-element.132) | copy-start | bytes 1966084
  2019.9 207.0 %all-gather.25.cloned.1.call-start = ((), (), s32[]{:S(2)}) async-start(), calls=%async_computation.24 | async-start | bytes 9830400 | tf_op jit(solution)/shard_map/all_gather | solution.py:23
  2101.8 208.8 %all-reduce.13.cloned.1.call-start = ((), (), s32[]{:S(2)}) async-start(), calls=%async_computation.28 | async-start | bytes 5242880 | tf_op jit(solution)/shard_map/psum | solution.py:283
  2235.4 171.2 %reduce-scatter.26.cloned.1.call-start = ((), (), s32[]{:S(2)}) async-start(), calls=%async_computation.25 | async-start | bytes 6553600 | tf_op jit(solution)/shard_map/reduce_scatter | solution.py:31
  2243.4 259.8 %reduce-scatter.16.cloned.1.call-start = ((), (), s32[]{:S(2)}) async-start(), calls=%async_computation.17 | async-start | bytes 6553600 | tf_op jit(solution)/shard_map/reduce_scatter | solution.py:31
  2257.3 375.4 %all-reduce.11.cloned.1.call-start = ((), (), s32[]{:S(2)}) async-start(), calls=%async_computation.27 | async-start | bytes 163840 | tf_op jit(solution)/shard_map/psum | solution.py:272
  2277.9 128.8 %copy-start.6 = (bf16[1,1024,320]{1,2,0:T(8,128)(2,1)S(1)}, bf16[1,1024,320]{1,2,0:T(8,128)(2,1)}, u32[]{:S(2)}) copy-start(bf16[1,1024,320]{1,2,0:T(8,128)(2,1)} %param.20) | copy-start | bytes 1966084
  2277.9 128.8 %copy-start.24 = (f32[1024]{0:T(1024)S(1)}, f32[1024]{0:T(1024)}, u32[]{:S(2)}) copy-start(f32[1024]{0:T(1024)} %copy-done.23) | copy-start | bytes 12292
  2277.9 128.8 %copy-start.26 = (f32[1024]{0:T(1024)S(1)}, f32[1024]{0:T(1024)}, u32[]{:S(2)}) copy-start(f32[1024]{0:T(1024)} %copy-done.25) | copy-start | bytes 12292
  2277.9 128.7 %copy-start.35 = (f32[320]{0:T(512)S(1)}, f32[320]{0:T(512)}, u32[]{:S(2)}) copy-start(f32[320]{0:T(512)} %param.25) | copy-start | bytes 3844
  2277.9 225.3 %copy-start.4 = (f32[1024,320]{0,1:T(8,128)S(1)}, f32[1024,320]{0,1:T(8,128)}, u32[]{:S(2)}) copy-start(f32[1024,320]{0,1:T(8,128)} %get-tuple-element.219) | copy-start | bytes 3932164
  2277.9 225.3 %copy-start.11 = (bf16[1,1024,320]{1,2,0:T(8,128)(2,1)S(1)}, bf16[1,1024,320]{1,2,0:T(8,128)(2,1)}, u32[]{:S(2)}) copy-start(bf16[1,1024,320]{1,2,0:T(8,128)(2,1)} %param.35) | copy-start | bytes 1966084
  2277.9 225.3 %copy-start.20 = (f32[1024]{0:T(1024)S(1)}, f32[1024]{0:T(1024)}, u32[]{:S(2)}) copy-start(f32[1024]{0:T(1024)} %copy-done.19) | copy-start | bytes 12292
  2277.9 225.3 %copy-start.22 = (f32[1024]{0:T(1024)S(1)}, f32[1024]{0:T(1024)}, u32[]{:S(2)}) copy-start(f32[1024]{0:T(1024)} %copy-done.21) | copy-start | bytes 12292
  2277.9 225.3 %copy-start.28 = (f32[1024]{0:T(1024)S(1)}, f32[1024]{0:T(1024)}, u32[]{:S(2)}) copy-start(f32[1024]{0:T(1024)} %copy-done.27) | copy-start | bytes 12292
  2277.9 225.3 %copy-start.30 = (f32[1024]{0:T(1024)S(1)}, f32[1024]{0:T(1024)}, u32[]{:S(2)}) copy-start(f32[1024]{0:T(1024)} %copy-done.29) | copy-start | bytes 12292
  2278.0 225.3 %copy-start.32 = (f32[320]{0:T(512)S(1)}, f32[320]{0:T(512)}, u32[]{:S(2)}) copy-start(f32[320]{0:T(512)} %param.27) | copy-start | bytes 3844
  2278.0 225.3 %copy-start.39 = (f32[320]{0:T(512)S(1)}, f32[320]{0:T(512)}, u32[]{:S(2)}) copy-start(f32[320]{0:T(512)} %param.32) | copy-start | bytes 3844
  2317.2 318.4 %copy-start.1 = (bf16[320,1280]{1,0:T(8,128)(2,1)S(1)}, bf16[320,1280]{1,0:T(8,128)(2,1)}, u32[]{:S(2)}) copy-start(bf16[320,1280]{1,0:T(8,128)(2,1)} %param.29) | copy-start | bytes 2457604
  2318.5 189.1 %copy-start.36 = (f32[320]{0:T(512)S(1)}, f32[320]{0:T(512)}, u32[]{:S(2)}) copy-start(f32[320]{0:T(512)} %get-tuple-element.141) | copy-start | bytes 3844
  2318.5 189.1 %copy-start.37 = (f32[320]{0:T(512)S(1)}, f32[320]{0:T(512)}, u32[]{:S(2)}) copy-start(f32[320]{0:T(512)} %get-tuple-element.147) | copy-start | bytes 3844
  (24 other events, 407.2 us)
Sparse Core Ops, SparseCore 0:
  19.8 53.1 all-gather.10
  84.8 120.4 reduce-scatter.9
  211.1 40.4 all-gather.12
  562.7 25.5 all-gather.14
  594.0 93.7 reduce-scatter.11
  689.2 53.4 all-gather.26
  744.9 53.5 all-gather.16
  801.1 153.7 reduce-scatter.17
  957.7 153.1 reduce-scatter.13
  1126.3 70.1 all-gather.20
  1209.3 93.7 reduce-scatter.19
  1316.1 52.5 all-gather.22
  1374.4 51.9 reduce-scatter.21
  2013.0 85.3 reduce-scatter.23
  2099.8 70.1 all-gather.18
  2171.6 55.3 all-gather.24
  2235.5 75.0 all-reduce.12
  2312.8 93.8 reduce-scatter.25
  2408.9 94.2 reduce-scatter.15
  2509.3 123.4 all-reduce.10
where the time goes:
time: 2660 us; the launch traced here: 2640 us
  waiting for transfers between devices  1470 us (55%)
  matrix products  398 us (15%)
  local copies, waits for them, and re-layouts  380 us (14%)
  other arithmetic  324 us (12%)
  blocking collectives  52.3 us (2%)
    reduce_scatter x5, waiting for transfers between devices, sum_over_row(): return lax.psum_scatter(values, 'row', scatter_dimension=0, tiled=True)  548 us
    reduce_scatter x4, waiting for transfers between devices, sum_over_col(): return lax.psum_scatter(values, 'col', scatter_dimension=0, tiled=True)  363 us
    add x8, local copies, waits for them, and re-layouts, head_scores(): rel_rows[:, :, :, None] + rel_cols[:, :, None, :]  223 us
    all_gather x4, waiting for transfers between devices, rows_over_row(): return lax.all_gather(values, 'row', axis=0, tiled=True)  202 us
    all_gather x4, waiting for transfers between devices, rows_over_col(): return lax.all_gather(values, 'col', axis=0, tiled=True)  193 us
    dot_general x8, matrix products, head_scores(): jnp.einsum('qc,kc->qk', query_one, key_one, preferred_element_type=jnp.fl...  124 us
    psum x1, waiting for transfers between devices, shards(): lax.psum((height_part, width_part), ('batch', 'row', 'col'))  106 us
    reshape x4, local copies, waits for them, and re-layouts, attend_back(): score_grad.astype(jnp.float32)  96.1 us
  transfers between devices with their start and end apart: 20, of which 20 were waited for; matrix products, arithmetic and copies ran while one was open for 5% of the time, Pallas kernels for 0%

commit v1 on v0

--- a/solution.py
+++ b/solution.py
@@ -3,6 +3,7 @@
 import jax.numpy as jnp
 from jax import lax
 from jax.sharding import PartitionSpec as P
+from jax.lax import all_to_all, axis_size
 
 D = 1280
 HEAD_DIM = 80
@@ -16,7 +17,15 @@
 
 
 def rows_over_col(values):
-    return lax.all_gather(values, "col", axis=0, tiled=True)
+    return jnp.concatenate(
+        all_to_all(
+            jnp.stack([values for _ in range(axis_size("col"))]),
+            axis_name="col",
+            split_axis=0,
+            concat_axis=0,
+        ),
+        axis=0,
+    )
 
 
 def rows_over_row(values):

time: 2660 us -> 2620 us (0.985)
  waiting for transfers between devices: 1470 us -> 1110 us
  blocking collectives: 52.3 us -> 367 us
    all_to_all x0 -> x4, blocking collectives: none -> 316 us  [rows_over_col(): all_to_all(jnp.stack([values for _ in range(axis_size('col'))]), axis_nam...]
    all_gather x4 -> x0, waiting for transfers between devices: 193 us -> none  [rows_over_col(): return lax.all_gather(values, 'col', axis=0, tiled=True)]
    reduce_scatter x4, waiting for transfers between devices: 363 us -> 273 us  [sum_over_col(): return lax.psum_scatter(values, 'col', scatter_dimension=0, tiled=True)]
    reduce_scatter x5, waiting for transfers between devices: 548 us -> 476 us  [sum_over_row(): return lax.psum_scatter(values, 'row', scatter_dimension=0, tiled=True)]
  transfers between devices with their start and end apart: 20 -> 16, of which waited for: 20 -> 16; matrix products, arithmetic and copies ran while one was open for 5% -> 5% of each run, Pallas kernels for 0% -> 0%
where the time goes in v1:
time: 2620 us; the launch traced here: 2600 us
  waiting for transfers between devices  1110 us (42%)
  local copies, waits for them, and re-layouts  397 us (15%)
  matrix products  388 us (15%)
  blocking collectives  367 us (14%)
  other arithmetic  321 us (12%)
    reduce_scatter x5, waiting for transfers between devices, sum_over_row(): return lax.psum_scatter(values, 'row', scatter_dimension=0, tiled=True)  476 us
    all_to_all x4, blocking collectives, rows_over_col(): all_to_all(jnp.stack([values for _ in range(axis_size('col'))]), axis_nam...  316 us
    reduce_scatter x4, waiting for transfers between devices, sum_over_col(): return lax.psum_scatter(values, 'col', scatter_dimension=0, tiled=True)  273 us
    add x8, local copies, waits for them, and re-layouts, head_scores(): rel_rows[:, :, :, None] + rel_cols[:, :, None, :]  223 us
    all_gather x4, waiting for transfers between devices, rows_over_row(): return lax.all_gather(values, 'row', axis=0, tiled=True)  202 us
    dot_general x8, matrix products, head_scores(): jnp.einsum('qc,kc->qk', query_one, key_one, preferred_element_type=jnp.fl...  124 us
    psum x1, waiting for transfers between devices, shards(): lax.psum((height_part, width_part), ('batch', 'row', 'col'))  106 us
    reshape x4, local copies, waits for them, and re-layouts, attend_back(): score_grad.astype(jnp.float32)  95.9 us
  transfers between devices with their start and end apart: 16, of which 16 were waited for; matrix products, arithmetic and copies ran while one was open for 5% of the time, Pallas kernels for 0%

profile of v1, /device:TPU:8, one launch (start us, length us, event | category | flops | bytes accessed | tf_op | source)
XLA Modules:
  0.0 2604.5 jit_solution(461979296085874811)
XLA Ops:
  19.1 61.5 %all_to_all.20 = bf16[4,1024,320]{1,2,0:T(8,128)(2,1)S(1)} all-to-all(bf16[4,1024,320]{1,2,0:T(8,128)(2,1)S(1)} %stack.47), channel_id=1, replica_groups=mesh['batch'=2,'row'=4,'col'=4] {'col'}, dimensions={0} | all-to-all | bytes 5242880 | tf_op jit(solution)/shard_map/all_to_all | solution.py:21
  98.6 119.8 %reduce-scatter.10.cloned.1.call-done = f32[1024,3,320]{0,2,1:T(8,128)} async-done(((f32[4096,3,320]{0,2,1:T(8,128)}), f32[1024,3,320]{0,2,1:T(8,128)}) %reduce-scatter.10.cloned.1.call-update) | async-done | bytes 3932176 | tf_op jit(solution)/shard_map/reduce_scatter | solution.py:36
  230.9 33.7 %all-gather.6.cloned.1.call-done = bf16[4096,2,320]{0,2,1:T(8,128)(2,1)} async-done(((bf16[1024,2,320]{0,2,1:T(8,128)(2,1)}), bf16[4096,2,320]{0,2,1:T(8,128)(2,1)}) %all-gather.6.cloned.1.call-update) | async-done | bytes 5242896 | tf_op jit(solution)/shard_map/all_gather | solution.py:45
  281.2 293.6 %while.30 = (s32[]{:T(128)}, bf16[4,1024,80]{1,2,0:T(8,128)(2,1)S(1)}, f32[4,1024]{1,0:T(4,128)}, bf16[4,1024,80]{2,1,0:T(8,128)(2,1)}, bf16[4,4096,80]{2,1,0:T(...) while((s32[]{:T(128)}, ...), condition=%wide.region_8.9_spmd, body=%wide.region_5.8_spmd.sunk | while | flops 1400978432 | bytes 123054200 | solution.py:159
  294.7 27.9 %add.332 = f32[1024,4096]{1,0:T(8,128)} reshape(f32[16,64,64,64]{3,2,1,0:T(8,128)} %broadcast_add_fusion.4) | data formatting | bytes 33554432 | tf_op jit(solution)/shard_map/while/body/eval_jaxpr/add | solution.py:82
  322.6 14.6 fusion.191
  368.1 27.9 %add.332 = f32[1024,4096]{1,0:T(8,128)} reshape(f32[16,64,64,64]{3,2,1,0:T(8,128)} %broadcast_add_fusion.4) | data formatting | bytes 33554432 | tf_op jit(solution)/shard_map/while/body/eval_jaxpr/add | solution.py:82
  396.0 14.6 fusion.191
  441.5 27.9 %add.332 = f32[1024,4096]{1,0:T(8,128)} reshape(f32[16,64,64,64]{3,2,1,0:T(8,128)} %broadcast_add_fusion.4) | data formatting | bytes 33554432 | tf_op jit(solution)/shard_map/while/body/eval_jaxpr/add | solution.py:82
  469.4 14.6 fusion.191
  514.9 27.9 %add.332 = f32[1024,4096]{1,0:T(8,128)} reshape(f32[16,64,64,64]{3,2,1,0:T(8,128)} %broadcast_add_fusion.4) | data formatting | bytes 33554432 | tf_op jit(solution)/shard_map/while/body/eval_jaxpr/add | solution.py:82
  542.8 14.6 fusion.191
  576.1 25.2 all-gather.8.cloned.1.call-done
  607.4 132.7 %all_to_all.21 = bf16[4,1024,320]{1,2,0:T(8,128)(2,1)S(1)} all-to-all(bf16[4,1024,320]{1,2,0:T(8,128)(2,1)S(1)} %stack.50), channel_id=1, replica_groups=mesh['batch'=2,'row'=4,'col'=4] {'col'}, dimensions={0} | all-to-all | bytes 5242880 | tf_op jit(solution)/shard_map/all_to_all | solution.py:21
  767.6 60.4 %all_to_all.22 = bf16[4,1024,320]{1,2,0:T(8,128)(2,1)S(1)} all-to-all(bf16[4,1024,320]{1,2,0:T(8,128)(2,1)S(1)} %stack.49), channel_id=1, replica_groups=mesh['batch'=2,'row'=4,'col'=4] {'col'}, dimensions={0} | all-to-all | bytes 5242880 | tf_op jit(solution)/shard_map/all_to_all | solution.py:21
  839.9 70.5 %reduce-scatter.18.cloned.1.call-done = f32[1024,1280]{1,0:T(8,128)} async-done(((f32[4096,1280]{1,0:T(8,128)}), f32[1024,1280]{1,0:T(8,128)}) %reduce-scatter.18.cloned.1.call-update) | async-done | bytes 5242896 | tf_op jit(solution)/shard_map/reduce_scatter | solution.py:36
  910.4 155.8 %reduce-scatter.14.cloned.1.call-done = f32[1024,1280]{1,0:T(8,128)} async-done(((f32[4096,1280]{1,0:T(8,128)}), f32[1024,1280]{1,0:T(8,128)}) %reduce-scatter.14.cloned.1.call-update) | async-done | bytes 5242896 | tf_op jit(solution)/shard_map/reduce_scatter | solution.py:36
  1066.2 15.2 add_convert_fusion
  1081.4 70.3 %all-gather.12.cloned.1.call-done = bf16[4096,1280]{1,0:T(8,128)(2,1)} async-done(((bf16[1024,1280]{1,0:T(8,128)(2,1)}), bf16[4096,1280]{1,0:T(8,128)(2,1)}) %all-gather.12.cloned.1.call-update) | async-done | bytes 10485776 | tf_op jit(solution)/shard_map/all_gather | solution.py:32
  1164.5 93.9 %reduce-scatter.20.cloned.1.call-done = f32[1024,320]{0,1:T(8,128)} async-done(((f32[4096,320]{0,1:T(8,128)}), f32[1024,320]{0,1:T(8,128)}) %reduce-scatter.20.cloned.1.call-update) | async-done | bytes 1310736 | tf_op jit(solution)/shard_map/reduce_scatter | solution.py:40
  1270.7 60.9 %all_to_all.23 = bf16[4,1024,320]{1,2,0:T(8,128)(2,1)S(1)} all-to-all(bf16[4,1024,320]{1,2,0:T(8,128)(2,1)S(1)} %stack.51), channel_id=1, replica_groups=mesh['batch'=2,'row'=4,'col'=4] {'col'}, dimensions={0} | all-to-all | bytes 5242880 | tf_op jit(solution)/shard_map/all_to_all | solution.py:21
  1338.9 51.8 %reduce-scatter.22.cloned.1.call-done = f32[1024,320]{0,1:T(8,128)} async-done(((f32[4096,320]{0,1:T(8,128)}), f32[1024,320]{0,1:T(8,128)}) %reduce-scatter.22.cloned.1.call-update) | async-done | bytes 1310736 | tf_op jit(solution)/shard_map/reduce_scatter | solution.py:36
  1393.4 574.2 %while.31 = (s32[]{:T(128)}, bf16[4,1024,80]{1,2,0:T(8,128)(2,1)}, f32[4,4096,80]{1,2,0:T(8,128)}, f32[4,4096,80]{1,2,0:T(8,128)}, f32[4,16,64,80]{3,2,1,0:T(8,1...) while((s32[]{:T(128)}, bf16[4,1024,80]{1,2,0:T(8,128)(2,1)}, ...), condition=%wide.region_27.28_spmd, body=%wide.region_23.27_spmd.sunk | while | flops 3678845952 | bytes 353068224 | solution.py:245
  1417.1 27.9 %add.339 = f32[1024,4096]{1,0:T(8,128)} reshape(f32[16,64,64,64]{3,2,1,0:T(8,128)} %broadcast_add_fusion.5) | data formatting | bytes 33554432 | tf_op jit(solution)/shard_map/while/body/eval_jaxpr/add | solution.py:82
  1445.0 16.5 multiply_reduce_fusion.7
  1484.3 24.0 reshape.200
  1508.3 15.4 fusion.216
  1560.5 27.9 %add.339 = f32[1024,4096]{1,0:T(8,128)} reshape(f32[16,64,64,64]{3,2,1,0:T(8,128)} %broadcast_add_fusion.5) | data formatting | bytes 33554432 | tf_op jit(solution)/shard_map/while/body/eval_jaxpr/add | solution.py:82
  1588.4 16.5 multiply_reduce_fusion.7
  1627.7 24.0 reshape.200
  1651.7 15.4 fusion.216
  1704.0 27.9 %add.339 = f32[1024,4096]{1,0:T(8,128)} reshape(f32[16,64,64,64]{3,2,1,0:T(8,128)} %broadcast_add_fusion.5) | data formatting | bytes 33554432 | tf_op jit(solution)/shard_map/while/body/eval_jaxpr/add | solution.py:82
  1731.9 16.5 multiply_reduce_fusion.7
  1771.2 24.0 reshape.200
  1795.1 15.4 fusion.216
  1847.3 27.9 %add.339 = f32[1024,4096]{1,0:T(8,128)} reshape(f32[16,64,64,64]{3,2,1,0:T(8,128)} %broadcast_add_fusion.5) | data formatting | bytes 33554432 | tf_op jit(solution)/shard_map/while/body/eval_jaxpr/add | solution.py:82
  1875.2 16.5 multiply_reduce_fusion.7
  1914.5 24.0 reshape.200
  1938.5 15.4 fusion.216
  1983.9 78.4 %reduce-scatter.24.cloned.1.call-done = f32[1024,2,320]{0,2,1:T(8,128)} async-done(((f32[4096,2,320]{0,2,1:T(8,128)}), f32[1024,2,320]{0,2,1:T(8,128)}) %reduce-scatter.24.cloned.1.call-update) | async-done | bytes 2621456 | tf_op jit(solution)/shard_map/reduce_scatter | solution.py:36
  2075.4 58.7 %all-gather.10.cloned.1.call-done = bf16[4096,1280]{1,0:T(8,128)(2,1)} async-done(((bf16[1024,1280]{1,0:T(8,128)(2,1)}), bf16[4096,1280]{1,0:T(8,128)(2,1)}) %all-gather.10.cloned.1.call-update) | async-done | bytes 10485776 | tf_op jit(solution)/shard_map/all_gather | solution.py:32
  2143.7 47.3 %all-gather.14.cloned.1.call-done = bf16[4096,3,320]{0,2,1:T(8,128)(2,1)} async-done(((bf16[1024,3,320]{0,2,1:T(8,128)(2,1)}), bf16[4096,3,320]{0,2,1:T(8,128)(2,1)}) %all-gather.14.cloned.1.call-update) | async-done | bytes 7864336 | tf_op jit(solution)/shard_map/all_gather | solution.py:32
  2207.0 12.8 fusion.105
  2249.7 23.3 all-reduce.13.cloned.1.call-done
  2280.9 88.2 %reduce-scatter.26.cloned.1.call-done = f32[1024,320]{0,1:T(8,128)} async-done(((f32[4096,320]{0,1:T(8,128)}), f32[1024,320]{0,1:T(8,128)}) %reduce-scatter.26.cloned.1.call-update) | async-done | bytes 1310736 | tf_op jit(solution)/shard_map/reduce_scatter | solution.py:40
  2378.0 87.5 %reduce-scatter.16.cloned.1.call-done = f32[1024,320]{0,1:T(8,128)} async-done(((f32[4096,320]{0,1:T(8,128)}), f32[1024,320]{0,1:T(8,128)}) %reduce-scatter.16.cloned.1.call-update) | async-done | bytes 1310736 | tf_op jit(solution)/shard_map/reduce_scatter | solution.py:40
  2469.9 19.1 all-reduce.1
  2489.0 106.0 %all-reduce.11.cloned.1.call-done = (f32[127,80]{0,1:T(8,128)}, f32[127,80]{0,1:T(8,128)}) async-done(((f32[127,80]{0,1:T(8,128)}, f32[127,80]{0,1:T(8,128)}), (f32[127,80]{0,1:T(8,128)}, f32[127,80]{0,1:T(8,128)})) %all-reduce.11.cloned.1.call-update) | async-done | bytes 81296 | tf_op jit(solution)/shard_map/psum | solution.py:281
  (341 shorter events, 611.0 us)
Async XLA Ops:
  7.2 822.7 %copy-start = (bf16[320,1280]{1,0:T(8,128)(2,1)S(1)}, bf16[320,1280]{1,0:T(8,128)(2,1)}, u32[]{:S(2)}) copy-start(bf16[320,1280]{1,0:T(8,128)(2,1)} %param.29) | copy-start | bytes 2457604
  7.2 211.2 %reduce-scatter.10.cloned.1.call-start = ((), (), s32[]{:S(2)}) async-start(), calls=%async_computation.13 | async-start | bytes 19660800 | tf_op jit(solution)/shard_map/reduce_scatter | solution.py:36
  97.9 126.5 %copy-start.53 = (bf16[127,80]{0,1:T(8,128)(2,1)S(1)}, bf16[127,80]{0,1:T(8,128)(2,1)}, u32[]{:S(2)}) copy-start(bf16[127,80]{0,1:T(8,128)(2,1)} %param.33) | copy-start | bytes 60964
  97.9 126.8 %copy-start.54 = (bf16[127,80]{0,1:T(8,128)(2,1)S(1)}, bf16[127,80]{0,1:T(8,128)(2,1)}, u32[]{:S(2)}) copy-start(bf16[127,80]{0,1:T(8,128)(2,1)} %param.34) | copy-start | bytes 60964
  97.9 166.7 %all-gather.6.cloned.1.call-start = ((), (), s32[]{:S(2)}) async-start(), calls=%async_computation.14 | async-start | bytes 6553600 | tf_op jit(solution)/shard_map/all_gather | solution.py:45
  224.0 377.3 %all-gather.8.cloned.1.call-start = ((), (), s32[]{:S(2)}) async-start(), calls=%async_computation.15 | async-start | bytes 3276800 | tf_op jit(solution)/shard_map/all_gather | solution.py:32
  224.4 45.7 %copy-start.51 = (s32[16]{0:T(128)}, s32[16]{0:T(128)S(1)}, u32[]{:S(2)}) copy-start(s32[16]{0:T(128)S(1)} %iota_add_fusion) | copy-start | bytes 196
  281.2 320.2 %copy-start.21 = (bf16[320,320]{1,0:T(8,128)(2,1)S(1)}, bf16[320,320]{1,0:T(8,128)(2,1)}, u32[]{:S(2)}) copy-start(bf16[320,320]{1,0:T(8,128)(2,1)} %param.23) | copy-start | bytes 614404
  575.6 31.4 %copy-start.17 = (bf16[1,1024,320]{1,2,0:T(8,128)(2,1)S(1)}, bf16[1,1024,320]{1,2,0:T(8,128)(2,1)}, u32[]{:S(2)}) copy-start(bf16[1,1024,320]{1,2,0:T(8,128)(2,1)} %param.35) | copy-start | bytes 1966084
  575.6 181.0 %reduce-scatter.12.cloned.1.call-start = ((), (), s32[]{:S(2)}) async-start(), calls=%async_computation.16 | async-start | bytes 6553600 | tf_op jit(solution)/shard_map/reduce_scatter | solution.py:40
  607.0 303.4 %reduce-scatter.18.cloned.1.call-start = ((), (), s32[]{:S(2)}) async-start(), calls=%async_computation.20 | async-start | bytes 26214400 | tf_op jit(solution)/shard_map/reduce_scatter | solution.py:36
  607.4 136.0 %copy-start.23 = (bf16[1280,320]{0,1:T(8,128)(2,1)S(1)}, bf16[1280,320]{0,1:T(8,128)(2,1)}, u32[]{:S(2)}) copy-start(bf16[1280,320]{0,1:T(8,128)(2,1)} %param.31) | copy-start | bytes 2457604
  753.4 312.7 %reduce-scatter.14.cloned.1.call-start = ((), (), s32[]{:S(2)}) async-start(), calls=%async_computation.17 | async-start | bytes 26214400 | tf_op jit(solution)/shard_map/reduce_scatter | solution.py:36
  765.4 502.8 %copy-start.28 = (f32[1024]{0:T(1024)}, f32[1024]{0:T(1024)S(1)}, u32[]{:S(2)}) copy-start(f32[1024]{0:T(1024)S(1)} %get-tuple-element.230) | copy-start | bytes 12292
  765.4 502.8 %copy-start.30 = (f32[1024]{0:T(1024)}, f32[1024]{0:T(1024)S(1)}, u32[]{:S(2)}) copy-start(f32[1024]{0:T(1024)S(1)} %get-tuple-element.231) | copy-start | bytes 12292
  839.8 226.4 %copy-start.42 = (f32[1280]{0:T(1024)S(1)}, f32[1280]{0:T(1024)}, u32[]{:S(2)}) copy-start(f32[1280]{0:T(1024)} %param.30) | copy-start | bytes 15364
  839.8 311.9 %all-gather.12.cloned.1.call-start = ((), (), s32[]{:S(2)}) async-start(), calls=%async_computation.21 | async-start | bytes 13107200 | tf_op jit(solution)/shard_map/all_gather | solution.py:32
  1081.4 176.9 %reduce-scatter.20.cloned.1.call-start = ((), (), s32[]{:S(2)}) async-start(), calls=%async_computation.22 | async-start | bytes 6553600 | tf_op jit(solution)/shard_map/reduce_scatter | solution.py:40
  1164.4 103.8 %copy-start.18 = (bf16[1,1024,320]{1,2,0:T(8,128)(2,1)S(1)}, bf16[1,1024,320]{1,2,0:T(8,128)(2,1)}, u32[]{:S(2)}) copy-start(bf16[1,1024,320]{1,2,0:T(8,128)(2,1)} %param.35) | copy-start | bytes 1966084
  1164.4 226.3 %reduce-scatter.22.cloned.1.call-start = ((), (), s32[]{:S(2)}) async-start(), calls=%async_computation.23 | async-start | bytes 6553600 | tf_op jit(solution)/shard_map/reduce_scatter | solution.py:36
  1268.1 63.5 %copy-start.36 = (f32[1024]{0:T(1024)}, f32[1024]{0:T(1024)S(1)}, u32[]{:S(2)}) copy-start(f32[1024]{0:T(1024)S(1)} %get-tuple-element.234) | copy-start | bytes 12292
  1268.2 63.5 %copy-start.38 = (f32[1024]{0:T(1024)}, f32[1024]{0:T(1024)S(1)}, u32[]{:S(2)}) copy-start(f32[1024]{0:T(1024)S(1)} %get-tuple-element.235) | copy-start | bytes 12292
  1338.8 723.5 %reduce-scatter.24.cloned.1.call-start = ((), (), s32[]{:S(2)}) async-start(), calls=%async_computation.24 | async-start | bytes 13107200 | tf_op jit(solution)/shard_map/reduce_scatter | solution.py:36
  1976.8 157.3 %all-gather.10.cloned.1.call-start = ((), (), s32[]{:S(2)}) async-start(), calls=%async_computation.18 | async-start | bytes 13107200 | tf_op jit(solution)/shard_map/all_gather | solution.py:32
  1983.8 80.4 %copy-start.27 = (bf16[4,1024,80]{1,2,0:T(8,128)(2,1)S(1)}, bf16[4,1024,80]{1,2,0:T(8,128)(2,1)}, u32[]{:S(2)}) copy-start(bf16[4,1024,80]{1,2,0:T(8,128)(2,1)} %get-tuple-element.132) | copy-start | bytes 1966084
  1983.8 207.1 %all-gather.14.cloned.1.call-start = ((), (), s32[]{:S(2)}) async-start(), calls=%async_computation.25 | async-start | bytes 9830400 | tf_op jit(solution)/shard_map/all_gather | solution.py:32
  2065.7 68.4 %copy-start.12 = (bf16[4,40,8,1024]{3,2,0,1:T(8,128)(2,1)S(1)}, bf16[4,40,8,1024]{3,2,0,1:T(8,128)(2,1)}, u32[]{:S(2)}) copy-start(bf16[4,40,8,1024]{3,2,0,1:T(8,128)(2,1)} %copy-done.11) | copy-start | bytes 7864324
  2065.7 207.3 %all-reduce.13.cloned.1.call-start = ((), (), s32[]{:S(2)}) async-start(), calls=%async_computation.28 | async-start | bytes 5242880 | tf_op jit(solution)/shard_map/psum | solution.py:292
  2141.5 49.5 %copy-start.16 = (bf16[4096,320,1]{0,1,2:T(8,128)(2,1)S(1)}, bf16[4096,320,1]{0,1,2:T(8,128)(2,1)}, u32[]{:S(2)}) copy-start(bf16[4096,320,1]{0,1,2:T(8,128)(2,1)} %reshape.190) | copy-start | bytes 7864324
  2143.7 54.2 %copy-start.25 = (bf16[320,3,320]{2,0,1:T(8,128)(2,1)S(1)}, bf16[320,3,320]{2,0,1:T(8,128)(2,1)}, u32[]{:S(2)}) copy-start(bf16[320,3,320]{2,0,1:T(8,128)(2,1)} %param.21) | copy-start | bytes 1843204
  2197.9 171.2 %reduce-scatter.26.cloned.1.call-start = ((), (), s32[]{:S(2)}) async-start(), calls=%async_computation.26 | async-start | bytes 6553600 | tf_op jit(solution)/shard_map/reduce_scatter | solution.py:40
  2205.9 259.7 %reduce-scatter.16.cloned.1.call-start = ((), (), s32[]{:S(2)}) async-start(), calls=%async_computation.19 | async-start | bytes 6553600 | tf_op jit(solution)/shard_map/reduce_scatter | solution.py:40
  2219.8 375.2 %all-reduce.11.cloned.1.call-start = ((), (), s32[]{:S(2)}) async-start(), calls=%async_computation.27 | async-start | bytes 163840 | tf_op jit(solution)/shard_map/psum | solution.py:281
  2241.8 127.3 %copy-start.6 = (bf16[1,1024,320]{1,2,0:T(8,128)(2,1)S(1)}, bf16[1,1024,320]{1,2,0:T(8,128)(2,1)}, u32[]{:S(2)}) copy-start(bf16[1,1024,320]{1,2,0:T(8,128)(2,1)} %param.20) | copy-start | bytes 1966084
  2241.8 127.3 %copy-start.33 = (f32[1024]{0:T(1024)S(1)}, f32[1024]{0:T(1024)}, u32[]{:S(2)}) copy-start(f32[1024]{0:T(1024)} %copy-done.32) | copy-start | bytes 12292
  2241.8 127.3 %copy-start.35 = (f32[1024]{0:T(1024)S(1)}, f32[1024]{0:T(1024)}, u32[]{:S(2)}) copy-start(f32[1024]{0:T(1024)} %copy-done.34) | copy-start | bytes 12292
  2241.8 127.3 %copy-start.44 = (f32[320]{0:T(512)S(1)}, f32[320]{0:T(512)}, u32[]{:S(2)}) copy-start(f32[320]{0:T(512)} %param.25) | copy-start | bytes 3844
  2241.8 223.7 %copy-start.4 = (f32[1024,320]{0,1:T(8,128)S(1)}, f32[1024,320]{0,1:T(8,128)}, u32[]{:S(2)}) copy-start(f32[1024,320]{0,1:T(8,128)} %get-tuple-element.219) | copy-start | bytes 3932164
  2241.8 223.7 %copy-start.19 = (bf16[1,1024,320]{1,2,0:T(8,128)(2,1)S(1)}, bf16[1,1024,320]{1,2,0:T(8,128)(2,1)}, u32[]{:S(2)}) copy-start(bf16[1,1024,320]{1,2,0:T(8,128)(2,1)} %param.35) | copy-start | bytes 1966084
  2241.9 223.7 %copy-start.29 = (f32[1024]{0:T(1024)S(1)}, f32[1024]{0:T(1024)}, u32[]{:S(2)}) copy-start(f32[1024]{0:T(1024)} %copy-done.28) | copy-start | bytes 12292
  2241.9 223.7 %copy-start.31 = (f32[1024]{0:T(1024)S(1)}, f32[1024]{0:T(1024)}, u32[]{:S(2)}) copy-start(f32[1024]{0:T(1024)} %copy-done.30) | copy-start | bytes 12292
  2241.9 223.7 %copy-start.37 = (f32[1024]{0:T(1024)S(1)}, f32[1024]{0:T(1024)}, u32[]{:S(2)}) copy-start(f32[1024]{0:T(1024)} %copy-done.36) | copy-start | bytes 12292
  2241.9 223.7 %copy-start.39 = (f32[1024]{0:T(1024)S(1)}, f32[1024]{0:T(1024)}, u32[]{:S(2)}) copy-start(f32[1024]{0:T(1024)} %copy-done.38) | copy-start | bytes 12292
  2241.9 223.7 %copy-start.41 = (f32[320]{0:T(512)S(1)}, f32[320]{0:T(512)}, u32[]{:S(2)}) copy-start(f32[320]{0:T(512)} %param.27) | copy-start | bytes 3844
  2241.9 223.7 %copy-start.48 = (f32[320]{0:T(512)S(1)}, f32[320]{0:T(512)}, u32[]{:S(2)}) copy-start(f32[320]{0:T(512)} %param.32) | copy-start | bytes 3844
  2279.6 318.2 %copy-start.1 = (bf16[320,1280]{1,0:T(8,128)(2,1)S(1)}, bf16[320,1280]{1,0:T(8,128)(2,1)}, u32[]{:S(2)}) copy-start(bf16[320,1280]{1,0:T(8,128)(2,1)} %param.29) | copy-start | bytes 2457604
  2280.9 189.0 %copy-start.45 = (f32[320]{0:T(512)S(1)}, f32[320]{0:T(512)}, u32[]{:S(2)}) copy-start(f32[320]{0:T(512)} %get-tuple-element.141) | copy-start | bytes 3844
  2280.9 189.0 %copy-start.46 = (f32[320]{0:T(512)S(1)}, f32[320]{0:T(512)}, u32[]{:S(2)}) copy-start(f32[320]{0:T(512)} %get-tuple-element.147) | copy-start | bytes 3844
  (29 other events, 154.4 us)
Sparse Core Ops, SparseCore 0:
  98.0 120.2 reduce-scatter.9
  224.2 40.4 all-gather.5
  575.8 25.5 all-gather.7
  607.1 149.4 reduce-scatter.11
  759.1 151.2 reduce-scatter.17
  913.0 153.1 reduce-scatter.13
  1081.5 70.1 all-gather.11
  1164.5 93.7 reduce-scatter.19
  1338.9 51.7 reduce-scatter.21
  1976.9 85.2 reduce-scatter.23
  2063.9 70.1 all-gather.9
  2135.6 55.3 all-gather.13
  2198.0 75.0 all-reduce.12
  2275.2 93.7 reduce-scatter.25
  2371.2 94.2 reduce-scatter.15
  2471.6 123.3 all-reduce.10
